TPU v7x, 32 devices: a whole 2x2x4 slice. The times are simulated.
32 devices in a mesh: chan: 16 (over z, y, x), day: 2 (over core).
Axes of the slice: x: 2, y: 2, z: 4, core: 2. Of those that a mesh axis runs over, the one named last changes fastest.
Arguments:
- spectra: bfloat16 [512, 64, 400], P('chan', 'day'), may hold values from -6 to 6
- owners: int32 [2], replicated, may hold values from 0 to 15
Outputs:
- stacks: bfloat16 [2, 512, 32, 400], P(None, ('chan', 'day'))
Inputs may be any that keep to these rules, and one draw needn't show every extreme that they name: `owners`: block indices along the channel axis; two steps may name the same block.
All inputs are finite; a program needn't handle non-finite values.
Results may differ from a plain program's by a relative error of at most 0.0073.
Values may be sent and summed in bfloat16 or wider, within the bound.
A program may use at most 64 MiB of HBM per device.

v0:
```python
import math
import jax
import jax.numpy as jnp
from jax import lax
from jax.sharding import PartitionSpec as P

LAGS = 400
STEPS = 2


def broadcast(array, axis, root):
    mine = lax.axis_index(axis) == root
    return lax.psum(jnp.where(mine, array, jnp.zeros_like(array)), axis)


def whiten(spectra, bins):
    values = spectra.astype(jnp.float32)
    real_part = values[..., :bins]
    imag_part = values[..., bins:]
    power = real_part * real_part + imag_part * imag_part
    mean_power = jnp.mean(power, axis=-1, keepdims=True)
    factor = lax.rsqrt(power + 0.25 * mean_power + 1e-06)
    return jnp.concatenate([real_part * factor, imag_part * factor], axis=-1).astype(jnp.bfloat16)


def lag_table(bins, lag_count):
    freqs = jnp.arange(bins, dtype=jnp.int32)
    shifts = jnp.arange(lag_count, dtype=jnp.int32) - lag_count // 2
    phase = jnp.mod(freqs[:, None] * shifts[None, :], 2 * bins)
    angle = phase.astype(jnp.float32) * (math.pi / bins)
    return jnp.concatenate([jnp.cos(angle), -jnp.sin(angle)], axis=0).astype(jnp.bfloat16)


def day_cross(own, other, bins):
    own_re, own_im = (own[..., :bins], own[..., bins:])
    oth_re, oth_im = (other[..., :bins], other[..., bins:])
    cross_re = jnp.einsum("iwf,jwf->ijf", own_re, oth_re, preferred_element_type=jnp.float32)
    cross_re = cross_re + jnp.einsum(
        "iwf,jwf->ijf", own_im, oth_im, preferred_element_type=jnp.float32
    )
    cross_im = jnp.einsum("iwf,jwf->ijf", own_im, oth_re, preferred_element_type=jnp.float32)
    cross_im = cross_im - jnp.einsum(
        "iwf,jwf->ijf", own_re, oth_im, preferred_element_type=jnp.float32
    )
    cross = jnp.concatenate([cross_re, cross_im], axis=-1).astype(jnp.bfloat16)
    return cross.astype(jnp.float32)


def apply_lags(summed, table, norm):
    kept = summed.astype(jnp.bfloat16)
    rows = kept.shape[0] * kept.shape[1]
    lagged = (
        jnp.dot(kept.reshape(rows, kept.shape[2]), table, preferred_element_type=jnp.float32) * norm
    )
    return lagged.reshape(kept.shape[0], kept.shape[1], table.shape[1]).astype(jnp.bfloat16)


def local(spectra, owners):
    bins = spectra.shape[-1] // 2
    windows_all = spectra.shape[1] * lax.axis_size("day")
    white = whiten(spectra, bins)
    table = lag_table(bins, LAGS)
    norm = 1.0 / math.sqrt(windows_all * bins)
    result_steps = []
    for step in range(STEPS):
        block = broadcast(white, "chan", owners[step])
        crossed = day_cross(white, block, bins)
        summed = lax.psum_scatter(
            crossed.astype(jnp.bfloat16), "day", scatter_dimension=0, tiled=True
        ).astype(jnp.float32)
        result_steps.append(apply_lags(summed, table, norm))
    return jnp.stack(result_steps, axis=0)


def solution(mesh):
    placed = (P("chan", "day", None), P())
    return jax.shard_map(
        local,
        mesh=mesh,
        in_specs=placed,
        out_specs=P(None, ("chan", "day"), None, None),
        check_vma=False,
    )
```

profile of v0, /device:TPU:0, one launch (start us, length us, event | category | flops | bytes accessed | tf_op | source)
XLA Modules:
  0.0 300.6 jit_solution(8346272925173790976)
XLA Ops:
  6.5 0.0 all-reduce.3.cloned.1.call-start
  6.5 1.5 convert_element_type.46
  8.0 0.5 fusion.13
  8.6 0.6 multiply_convert_fusion.1
  9.2 0.0 copy-start.11
  9.2 0.0 copy-start.14
  9.2 0.8 copy-done.11
  10.0 0.2 copy-done.12
  10.2 1.4 pad_maximum_fusion
  11.6 3.7 %copy.11 = bf16[32,32,400]{1,0,2:T(8,128)(2,1)S(1)} copy(bf16[32,32,400]{2,1,0:T(8,128)(2,1)} %pad_maximum_fusion) | data formatting | bytes 1638400 | tf_op jit(solution)/shard_map/concatenate | solution.py:23
  15.3 0.7 fusion.14
  17.3 3.2 %broadcast_select_fusion.1 = (bf16[32,32,400]{1,0,2:T(8,128)(2,1)}, bf16[32,32,400]{1,0,2:T(8,128)(2,1)}) fusion(bf16[32,32,400]{1,0,2:T(8,128)(2,1)S(1)} %copy.11, pred[]{:T(512)S(6)} %eq.8, pred[]{:T(512)S(6)} %eq.9), kind=kLoop, calls=%fused_computation.5 | loop fusion | flops 819200 | bytes 2457602 | tf_op jit(solution)/shard_map/jit(_where)/select_n | solution.py:13
  20.4 0.0 all-reduce.3.cloned.1.call-update
  20.4 0.0 reduce-scatter.3.cloned.1.call-start
  20.5 1.0 copy-done.13
  21.5 1.5 copy.12
  22.9 0.0 copy-start.4
  23.0 2.6 copy.13
  25.5 0.0 copy-start.6
  25.5 213.4 %all-reduce.3.cloned.1.call-done = (bf16[32,32,400]{1,0,2:T(8,128)(2,1)}, bf16[32,32,400]{1,0,2:T(8,128)(2,1)}) async-done(((bf16[32,32,400]{1,0,2:T(8,128)(2,1)}, bf16[32,32,400]{1,0,2:T(8,128)(2,1)}), (bf16[32,32,400]{1,0,2:T(8,128)(2,1)}, bf16[32,32,400]{1,0,2:T(8,128)(2,1)})) %all-reduce.3.cloned.1.call-update) | async-done | bytes 1638416 | tf_op jit(solution)/shard_map/psum | solution.py:13
  238.9 4.2 %fusion.15 = f32[200,32,32]{2,1,0:T(8,128)} fusion(bf16[32,32,400]{1,0,2:T(8,128)(2,1)} %get-tuple-element.6, bf16[32,32,200]{1,0,2:T(8,128)(2,1)S(1)} %copy.12), kind=kOutput, calls=%fused_computation.38 | convolution fusion | flops 13107200 | bytes 2048000 | tf_op jit(solution)/shard_map/iwf,jwf->ijf/dot_general | solution.py:37
  243.2 0.0 copy-done.2
  243.2 2.7 fusion.16
  245.8 2.7 fusion.17
  248.6 2.7 fusion.18
  251.3 0.0 copy-done.3
  251.3 1.4 copy-done.9
  252.7 2.1 fusion
  254.8 3.8 %copy.16 = bf16[32,32,200]{2,1,0:T(8,128)(2,1)} copy(bf16[32,32,200]{0,1,2:T(8,128)(2,1)} %fusion) | data formatting | bytes 819200 | tf_op jit(solution)/shard_map/add | solution.py:38
  258.6 4.6 %fusion.1 = bf16[32,32,200]{0,1,2:T(8,128)(2,1)} fusion(f32[200,32,32]{2,1,0:T(8,128)} %fusion.16, bf16[32,32,400]{1,0,2:T(8,128)(2,1)S(1)} %copy-done.3, bf16[32,32,200]{1,0,2:T(8,128)(2,1)} %copy-done.4), kind=kOutput, calls=%fused_computation.7 | convolution fusion | flops 13516800 | bytes 2457600 | tf_op jit(solution)/shard_map/iwf,jwf->ijf/dot_general | solution.py:42
  263.2 4.0 %copy.17 = bf16[32,32,200]{2,1,0:T(8,128)(2,1)} copy(bf16[32,32,200]{0,1,2:T(8,128)(2,1)} %fusion.1) | data formatting | bytes 819200 | tf_op jit(solution)/shard_map/sub | solution.py:42
  267.2 2.6 pad_maximum_fusion.1
  269.8 0.0 reduce-scatter.3.cloned.1.call-update
  269.8 0.2 reduce-scatter.5.cloned.1.call-start
  270.1 4.7 %fusion.2 = bf16[32,32,200]{0,1,2:T(8,128)(2,1)} fusion(f32[200,32,32]{2,1,0:T(8,128)} %fusion.17, bf16[32,32,400]{1,0,2:T(8,128)(2,1)S(1)} %copy-done.1, bf16[32,32,200]{1,0,2:T(8,128)(2,1)} %copy-done.6), kind=kOutput, calls=%fused_computation.8 | convolution fusion | flops 13516800 | bytes 2457600 | tf_op jit(solution)/shard_map/iwf,jwf->ijf/dot_general | solution.py:38
  274.8 2.1 fusion.3
  276.9 3.3 %copy.24 = bf16[32,32,200]{2,1,0:T(8,128)(2,1)S(1)} copy(bf16[32,32,200]{0,1,2:T(8,128)(2,1)} %fusion.2) | data formatting | bytes 819200 | tf_op jit(solution)/shard_map/add | solution.py:38
  280.3 1.9 copy.25
  282.1 1.4 pad_maximum_fusion.2
  283.5 0.0 reduce-scatter.5.cloned.1.call-update
  283.6 1.8 cosine_convert_fusion
  285.3 0.0 reduce-scatter.3.cloned.1.call-done
  285.4 1.5 fusion.4
  286.8 0.2 copy.18
  287.1 4.2 %reduce-scatter.5.cloned.1.call-done = bf16[16,32,400]{2,1,0:T(8,128)(2,1)} async-done(((bf16[32,32,400]{2,1,0:T(8,128)(2,1)}), bf16[16,32,400]{2,1,0:T(8,128)(2,1)}) %reduce-scatter.5.cloned.1.call-update) | async-done | bytes 409616 | tf_op jit(solution)/shard_map/reduce_scatter | solution.py:68
  291.2 1.5 fusion.5
  292.7 0.2 copy.26
  292.9 1.1 pad_maximum_fusion.3
  (22 shorter events, 0.0 us)
Async XLA Ops:
  6.5 232.4 %all-reduce.3.cloned.1.call-start = ((), (), s32[]{:S(2)}) async-start(), calls=%async_computation.4 | async-start | bytes 13107200 | tf_op jit(solution)/shard_map/psum | solution.py:13
  9.2 0.8 copy-start.11
  9.2 1.0 copy-start.12
  9.2 6.0 %copy-start.14 = (s32[2]{0:T(128)S(1)}, s32[2]{0:T(128)}, u32[]{:S(2)}) copy-start(s32[2]{0:T(128)} %param.3) | copy-start | bytes 28
  20.4 1.0 copy-start.13
  20.4 264.9 %reduce-scatter.3.cloned.1.call-start = ((), (), s32[]{:S(2)}) async-start(), calls=%async_computation.2 | async-start | bytes 1572864 | tf_op jit(solution)/shard_map/reduce_scatter | solution.py:68
  22.9 222.9 %copy-start.4 = (bf16[32,32,200]{1,0,2:T(8,128)(2,1)}, bf16[32,32,200]{1,0,2:T(8,128)(2,1)S(1)}, u32[]{:S(2)}) copy-start(bf16[32,32,200]{1,0,2:T(8,128)(2,1)S(1)} %copy.12) | copy-start | bytes 1228804
  25.5 217.6 %copy-start.6 = (bf16[32,32,200]{1,0,2:T(8,128)(2,1)}, bf16[32,32,200]{1,0,2:T(8,128)(2,1)S(1)}, u32[]{:S(2)}) copy-start(bf16[32,32,200]{1,0,2:T(8,128)(2,1)S(1)} %copy.13) | copy-start | bytes 1228804
  238.9 4.2 %copy-start.2 = (bf16[32,32,400]{1,0,2:T(8,128)(2,1)S(1)}, bf16[32,32,400]{1,0,2:T(8,128)(2,1)}, u32[]{:S(2)}) copy-start(bf16[32,32,400]{1,0,2:T(8,128)(2,1)} %get-tuple-element.6) | copy-start | bytes 2457604
  243.2 2.7 copy-start
  245.8 2.7 copy-start.7
  248.5 2.7 copy-start.3
  248.5 4.1 %copy-start.9 = (f32[200,32,32]{2,1,0:T(8,128)S(1)}, f32[200,32,32]{2,1,0:T(8,128)}, u32[]{:S(2)}) copy-start(f32[200,32,32]{2,1,0:T(8,128)} %fusion.15) | copy-start | bytes 2457604
  263.2 6.9 %copy-start.1 = (bf16[32,32,400]{1,0,2:T(8,128)(2,1)S(1)}, bf16[32,32,400]{1,0,2:T(8,128)(2,1)}, u32[]{:S(2)}) copy-start(bf16[32,32,400]{1,0,2:T(8,128)(2,1)} %get-tuple-element.5) | copy-start | bytes 2457604
  269.8 21.4 %reduce-scatter.5.cloned.1.call-start = ((), (), s32[]{:S(2)}) async-start(), calls=%async_computation.3 | async-start | bytes 1572864 | tf_op jit(solution)/shard_map/reduce_scatter | solution.py:68
  270.0 4.7 %copy-start.5 = (bf16[32,32,200]{1,0,2:T(8,128)(2,1)S(1)}, bf16[32,32,200]{1,0,2:T(8,128)(2,1)}, u32[]{:S(2)}) copy-start(bf16[32,32,200]{1,0,2:T(8,128)(2,1)} %copy-done.4) | copy-start | bytes 1228804
  270.1 4.7 %copy-start.8 = (f32[200,32,32]{2,1,0:T(8,128)S(1)}, f32[200,32,32]{2,1,0:T(8,128)}, u32[]{:S(2)}) copy-start(f32[200,32,32]{2,1,0:T(8,128)} %fusion.18) | copy-start | bytes 2457604
  276.9 3.3 %copy-start.10 = (bf16[32,32,200]{0,1,2:T(8,128)(2,1)S(1)}, bf16[32,32,200]{0,1,2:T(8,128)(2,1)}, u32[]{:S(2)}) copy-start(bf16[32,32,200]{0,1,2:T(8,128)(2,1)} %fusion.3) | copy-start | bytes 1228804
Sparse Core Ops, SparseCore 0:
  20.6 218.3 all-reduce.2
  269.9 7.4 reduce-scatter.2
  283.7 7.5 reduce-scatter.4
where the time goes:
time: 301 us
  waiting for transfers between devices  218 us (72%)
  matrix products  28.8 us (10%)
  local copies, waits for them, and re-layouts  25.2 us (8%)
  between operations  14.7 us (5%)
  other arithmetic  14 us (5%)
    psum x1, waiting for transfers between devices, broadcast(): return lax.psum(jnp.where(mine, array, jnp.zeros_like(array)), axis)  213 us
    add x2, local copies, waits for them, and re-layouts, day_cross(): cross_re + jnp.einsum('iwf,jwf->ijf', own_im, oth_im, preferred_element_t...  7.15 us
    dot_general x2, matrix products, day_cross(): jnp.einsum('iwf,jwf->ijf', own_re, oth_re, preferred_element_type=jnp.flo...  6.94 us
    dot_general x2, matrix products, day_cross(): jnp.einsum('iwf,jwf->ijf', own_im, oth_im, preferred_element_type=jnp.flo...  6.86 us
    dot_general x2, matrix products, day_cross(): jnp.einsum('iwf,jwf->ijf', own_re, oth_im, preferred_element_type=jnp.flo...  6.69 us
  transfers between devices with their start and end apart: 3, of which 2 were waited for; matrix products, arithmetic and copies ran while one was open for 7% of the time, Pallas kernels for 0%

commit v1 on v0

--- a/solution.py
+++ b/solution.py
@@ -8,9 +8,15 @@
 STEPS = 2
 
 
+def sums_all_report(field, which_axis):
+    far_arr = lax.all_gather(field, axis_name=which_axis)
+    now = jnp.sum(far_arr, 0)
+    return now
+
+
 def broadcast(array, axis, root):
     mine = lax.axis_index(axis) == root
-    return lax.psum(jnp.where(mine, array, jnp.zeros_like(array)), axis)
+    return sums_all_report(jnp.where(mine, array, jnp.zeros_like(array)), axis)
 
 
 def whiten(spectra, bins):

time: 301 us -> 450 us (1.50)
  waiting for transfers between devices: 218 us -> 346 us
  other arithmetic: 14 us -> 32.2 us
  local copies, waits for them, and re-layouts: 25.2 us -> 36.2 us
  matrix products: 28.8 us -> 20.5 us
    all_gather x0 -> x2, waiting for transfers between devices: none -> 342 us  [sums_all_report(): far_arr = lax.all_gather(field, axis_name=which_axis)]
    psum x1 -> x0, waiting for transfers between devices: 213 us -> none  [broadcast(): return lax.psum(jnp.where(mine, array, jnp.zeros_like(array)), axis)]
    reduce_sum x0 -> x2, other arithmetic: none -> 20.8 us  [sums_all_report(): now = jnp.sum(far_arr, 0)]
    unnamed x30 -> x18, local copies, waits for them, and re-layouts: 3.37 us -> 12.7 us
  transfers between devices with their start and end apart: 3 -> 4, of which waited for: 2 -> 3; matrix products, arithmetic and copies ran while one was open for 7% -> 18% of each run, Pallas kernels for 0% -> 0%
where the time goes in v1:
time: 450 us
  waiting for transfers between devices  346 us (77%)
  local copies, waits for them, and re-layouts  36.2 us (8%)
  other arithmetic  32.2 us (7%)
  matrix products  20.5 us (5%)
  between operations  14.6 us (3%)
    all_gather x2, waiting for transfers between devices, sums_all_report(): far_arr = lax.all_gather(field, axis_name=which_axis)  342 us
    reduce_sum x2, other arithmetic, sums_all_report(): now = jnp.sum(far_arr, 0)  20.8 us
    unnamed x18, local copies, waits for them, and re-layouts  12.7 us
  transfers between devices with their start and end apart: 4, of which 3 were waited for; matrix products, arithmetic and copies ran while one was open for 18% of the time, Pallas kernels for 0%

profile of v1, /device:TPU:0, one launch (start us, length us, event | category | flops | bytes accessed | tf_op | source)
XLA Modules:
  0.0 449.7 jit_solution(9655526149638644921)
XLA Ops:
  6.5 1.5 convert_element_type.61
  8.0 0.5 fusion.13
  8.6 0.0 copy-start.6
  8.6 0.6 multiply_convert_fusion.1
  9.2 0.0 copy-done.6
  9.2 0.7 fusion.16
  11.2 1.9 broadcast_select_fusion.1
  13.1 0.0 all-gather.3.cloned.1.call-update
  13.2 0.0 all-gather.5.cloned.1.call-start
  13.2 0.7 all-gather.5.cloned.1.call-update
  13.9 0.0 reduce-scatter.3.cloned.1.call-start
  14.0 1.5 copy.26
  15.5 2.4 copy.28
  17.9 189.2 %all-gather.3.cloned.1.call-done = bf16[16,32,32,400]{3,2,1,0:T(8,128)(2,1)} async-done(((bf16[1,32,32,400]{3,2,1,0:T(8,128)(2,1)}), bf16[16,32,32,400]{3,2,1,0:T(8,128)(2,1)}) %all-gather.3.cloned.1.call-update) | async-done | bytes 13107216 | tf_op jit(solution)/shard_map/all_gather | solution.py:12
  207.0 10.3 %reduce_sum.34 = bf16[32,32,400]{2,1,0:T(8,128)(2,1)} reduce(bf16[16,32,32,400]{3,2,1,0:T(8,128)(2,1)} %all-gather.3.cloned.1.call-done, bf16[]{:T(256)} %constant.32.clone.1), dimensions={0}, to_apply=%region_1.2 | reduce | flops 6144000 | bytes 13926402 | tf_op jit(solution)/shard_map/reduce_sum | solution.py:13
  217.4 2.5 fusion.14
  219.9 3.2 copy.43
  223.1 3.2 copy.44
  226.2 2.5 fusion.17
  228.8 2.2 fusion
  230.9 3.9 copy.31
  234.8 2.5 fusion.18
  237.4 2.2 fusion.1
  239.5 3.8 copy.32
  243.4 2.6 pad_maximum_fusion.1
  246.0 0.0 reduce-scatter.3.cloned.1.call-update
  246.0 0.2 reduce-scatter.5.cloned.1.call-start
  246.2 152.8 %all-gather.5.cloned.1.call-done = bf16[16,32,32,400]{3,2,1,0:T(8,128)(2,1)} async-done(((bf16[1,32,32,400]{3,2,1,0:T(8,128)(2,1)}), bf16[16,32,32,400]{3,2,1,0:T(8,128)(2,1)}) %all-gather.5.cloned.1.call-update) | async-done | bytes 13107216 | tf_op jit(solution)/shard_map/all_gather | solution.py:12
  399.0 10.5 %reduce_sum.35 = bf16[32,32,400]{2,1,0:T(8,128)(2,1)} reduce(bf16[16,32,32,400]{3,2,1,0:T(8,128)(2,1)} %all-gather.5.cloned.1.call-done, bf16[]{:T(256)} %constant.32.clone.1), dimensions={0}, to_apply=%region_3.4 | reduce | flops 6144000 | bytes 13926402 | tf_op jit(solution)/shard_map/reduce_sum | solution.py:13
  409.5 2.5 fusion.15
  412.0 3.2 copy.45
  415.1 3.2 copy.46
  418.3 2.5 fusion.19
  420.8 2.2 fusion.2
  423.0 3.8 copy.40
  426.9 2.5 fusion.20
  429.4 1.0 fusion.3
  430.4 1.9 copy.41
  432.3 1.4 pad_maximum_fusion.2
  433.7 0.0 reduce-scatter.5.cloned.1.call-update
  433.7 1.8 cosine_convert_fusion
  435.5 0.0 reduce-scatter.3.cloned.1.call-done
  435.5 1.5 fusion.4
  437.0 0.2 copy.33
  437.2 3.2 reduce-scatter.5.cloned.1.call-done
  440.4 1.5 fusion.5
  441.9 0.2 copy.42
  442.1 1.1 pad_maximum_fusion.3
  (15 shorter events, 0.0 us)
Async XLA Ops:
  6.5 200.5 %all-gather.3.cloned.1.call-start = ((), (), s32[]{:S(2)}) async-start(), calls=%async_computation.2 | async-start | bytes 17825792 | tf_op jit(solution)/shard_map/all_gather | solution.py:12
  8.6 0.7 copy-start.6
  9.2 4.0 copy-start.4
  13.2 385.8 %all-gather.5.cloned.1.call-start = ((), (), s32[]{:S(2)}) async-start(), calls=%async_computation.4 | async-start | bytes 17825792 | tf_op jit(solution)/shard_map/all_gather | solution.py:12
  13.9 421.5 %reduce-scatter.3.cloned.1.call-start = ((), (), s32[]{:S(2)}) async-start(), calls=%async_computation.3 | async-start | bytes 1572864 | tf_op jit(solution)/shard_map/reduce_scatter | solution.py:74
  226.2 2.5 copy-start.2
  234.8 2.5 copy-start.3
  246.0 194.4 %reduce-scatter.5.cloned.1.call-start = ((), (), s32[]{:S(2)}) async-start(), calls=%async_computation.5 | async-start | bytes 1572864 | tf_op jit(solution)/shard_map/reduce_scatter | solution.py:74
  418.3 2.5 copy-start
  426.8 2.5 copy-start.1
  430.4 1.9 copy-start.5
Sparse Core Ops, SparseCore 0:
  13.3 193.7 all-gather.2
  209.8 189.1 all-gather.4
  401.3 6.5 reduce-scatter.2
  433.8 6.5 reduce-scatter.4
